TPU v7x, 32 devices: a whole 2x2x4 slice. The times are simulated.
32 devices in a mesh: fsdp: 8 (over y, x, core), tp: 4 (over z).
Axes of the slice: x: 2, y: 2, z: 4, core: 2. Of those that a mesh axis runs over, the one named last changes fastest.
Arguments:
- features: bfloat16 [1024, 8192], P('fsdp'), may hold values from -17 to 17
- key_partials: bfloat16 [1024, 4, 128], P('fsdp', 'tp'), may hold values from -0.30935922 to 0.30935922
- momentum: float32 [4096, 4, 128], P('fsdp', 'tp'), may hold values from -6 to 6
Outputs:
- update: float32 [4096, 4, 128], P('fsdp', 'tp')
- new_momentum: float32 [4096, 4, 128], P('fsdp', 'tp')
All inputs are finite; a program needn't handle non-finite values.
Results may differ from a plain program's by a relative error of at most 0.0003.
Values may be sent and summed in bfloat16 or wider, within the bound.
No kernel may reach another device: no remote copies, remote signals or barrier semaphores. Data moves between devices by JAX's collectives and lax.ppermute only.
A program may use at most 64 MiB of HBM per device.

v0:
```python
import math
import jax
import jax.numpy as jnp
from jax import lax
from jax.sharding import PartitionSpec as P

D_W = 8192
ITERS = 5
retain = 0.95
first_coef = 3.4445
second_coef = -4.775
third_coef = 2.0315
epsilon = 1e-07
shrink = 0.2


def swapped(block, axis, distance):
    count = lax.axis_size(axis)
    route = []
    for low in range(count):
        high = low | 1 << distance
        if high != low and high < count:
            route += [(low, high), (high, low)]
    return lax.ppermute(block, axis, route)


def on_device(features, key_partials, momentum):
    precise = lax.Precision.HIGHEST
    contract = (((0,), (0,)), ((), ()))
    parity = lax.axis_index("tp") % 2
    own_part = key_partials[:, 0, :]
    head_size = key_partials.shape[2]
    rows_half = momentum.shape[0]
    shard = lax.psum_scatter(
        lax.dot_general(features, own_part, contract, preferred_element_type=jnp.float32),
        "fsdp",
        scatter_dimension=0,
        tiled=True,
    )
    pieces = shard.reshape(2, rows_half, head_size)
    mine = jnp.where(parity == 0, pieces[0], pieces[1])
    other = jnp.where(parity == 0, pieces[1], pieces[0])
    grads = mine + swapped(other, "tp", 0)
    moment = momentum[:, 0, :]
    fresh = retain * moment + grads
    blend = grads + retain * fresh
    gram = lax.dot_general(blend, blend, contract, precision=precise)
    gram = lax.psum(gram, "fsdp")
    gram = gram + swapped(gram, "tp", 0)
    inverse = 1.0 / (jnp.sqrt(jnp.trace(gram)) + epsilon)
    state = blend * inverse
    gram = gram * (inverse * inverse)
    identity = jnp.eye(head_size, dtype=jnp.float32)
    for step in range(ITERS):
        square = jnp.dot(gram, gram, precision=precise)
        poly = first_coef * identity + second_coef * gram + third_coef * square
        state = jnp.dot(state, poly, precision=precise)
        gram = jnp.dot(poly, jnp.dot(gram, poly, precision=precise), precision=precise)
    update = shrink * math.sqrt(D_W) * state
    return (update[:, None, :], fresh[:, None, :])


def solution(mesh):
    placed = (P("fsdp", None), P("fsdp", "tp", None), P("fsdp", "tp", None))
    return jax.shard_map(
        on_device,
        mesh=mesh,
        in_specs=placed,
        out_specs=(P("fsdp", "tp", None), P("fsdp", "tp", None)),
        check_vma=False,
    )
```

profile of v0, /device:TPU:0, one launch (start us, length us, event | category | flops | bytes accessed | tf_op | source)
XLA Modules:
  0.0 150.5 jit_solution(14905172062143592151)
XLA Ops:
  7.2 0.0 reduce-scatter.2.cloned.1.call-start
  7.2 1.5 %copy-done = bf16[128,8192]{1,0:T(8,128)(2,1)S(1)} copy-done((bf16[128,8192]{1,0:T(8,128)(2,1)S(1)}, bf16[128,8192]{1,0:T(8,128)(2,1)}, u32[]{:S(2)}) %copy-start) | copy-done | bytes 2097176
  8.8 3.4 %fusion.14 = f32[8192,128]{1,0:T(8,128)} fusion(bf16[128,8192]{1,0:T(8,128)(2,1)S(1)} %copy-done, bf16[128,1,128]{2,0,1:T(8,128)(2,1)} %param.4), kind=kOutput, calls=%fused_computation.29 | convolution fusion | flops 268435456 | bytes 6324224 | tf_op jit(solution)/shard_map/dot_general | solution.py:35
  12.2 0.0 all-reduce.2.cloned.1.call-start
  12.3 54.0 %reduce-scatter.2.cloned.1.call-done = f32[1024,128]{1,0:T(8,128)} async-done(((f32[8192,128]{1,0:T(8,128)}), f32[1024,128]{1,0:T(8,128)}) %reduce-scatter.2.cloned.1.call-update) | async-done | bytes 524304 | tf_op jit(solution)/shard_map/reduce_scatter | solution.py:34
  66.3 1.1 slice_select_fusion
  67.3 1.5 %collective-permute-start = (f32[512,128]{1,0:T(8,128)S(1)}, f32[512,128]{1,0:T(8,128)S(1)}, u32[]{:S(2)}, u32[]{:S(2)}) collective-permute-start(f32[512,128]{1,0:T(8,128)S(1)} %slice_select_fusion), channel_id=1, source_target_pairs={{0,1},{1,0},{2,3},{3,2},{4,5},{5,4},{6,7},{7,6},{8,9},{9,8},{10,11... | collective-permute-start | bytes 786440 | tf_op jit(solution)/shard_map/ppermute | solution.py:24
  68.9 6.4 %collective-permute-done = f32[512,128]{1,0:T(8,128)S(1)} collective-permute-done((f32[512,128]{1,0:T(8,128)S(1)}, f32[512,128]{1,0:T(8,128)S(1)}, u32[]{:S(2)}, u32[]{:S(2)}) %collective-permute-start) | collective-permute-done | bytes 262176 | tf_op jit(solution)/shard_map/ppermute | solution.py:24
  75.3 1.8 %bitcast_add_fusion = (f32[512,128]{1,0:T(8,128)}, f32[512,128]{1,0:T(8,128)S(1)}) fusion(f32[512,1,128]{2,0,1:T(8,128)S(1)} %bitcast.51, f32[512,128]{1,0:T(8,128)S(1)} %collective-permute-done, f32[1024,128]{1,0:T(8,128)} %reduce-scatter.2.cloned.1.call-done, pred[]{:T(512)S(6)} %eq.21), kind=kLoop, calls=%fused_computation.10 | loop fusion | flops 262144 | bytes 1572865 | tf_op jit(solution)/shard_map/add | solution.py:45
  77.1 1.2 fusion.7
  78.3 53.3 %all-reduce.2.cloned.1.call-done = f32[128,128]{1,0:T(8,128)} async-done(((f32[128,128]{1,0:T(8,128)}), f32[128,128]{1,0:T(8,128)}) %all-reduce.2.cloned.1.call-update) | async-done | bytes 65552 | tf_op jit(solution)/shard_map/psum | solution.py:48
  131.7 1.5 collective-permute-start.1
  133.2 3.0 %collective-permute-done.1 = f32[128,128]{1,0:T(8,128)S(1)} collective-permute-done((f32[128,128]{1,0:T(8,128)}, f32[128,128]{1,0:T(8,128)S(1)}, u32[]{:S(2)}, u32[]{:S(2)}) %collective-permute-start.1) | collective-permute-done | bytes 65568 | tf_op jit(solution)/shard_map/ppermute | solution.py:24
  136.2 1.5 select_reduce_fusion
  138.4 0.2 fusion.8
  138.6 0.4 fusion.4
  139.0 0.2 fusion.9
  139.2 0.2 fusion.20
  139.4 0.2 fusion.3
  139.6 0.2 fusion.22
  139.8 0.4 fusion.21
  140.2 0.2 fusion.23
  140.4 0.2 fusion.2
  140.6 0.2 fusion.25
  140.8 0.4 fusion.24
  141.2 0.2 fusion.26
  141.4 0.2 fusion.1
  141.6 0.2 fusion.28
  141.8 0.4 fusion.27
  142.2 0.2 fusion.29
  142.4 0.2 fusion
  142.6 1.1 convolution_multiply_fusion
  (5 shorter events, 0.0 us)
Async XLA Ops:
  7.2 1.6 %copy-start = (bf16[128,8192]{1,0:T(8,128)(2,1)S(1)}, bf16[128,8192]{1,0:T(8,128)(2,1)}, u32[]{:S(2)}) copy-start(bf16[128,8192]{1,0:T(8,128)(2,1)} %param.3) | copy-start | bytes 6291460
  7.2 59.1 %reduce-scatter.2.cloned.1.call-start = ((), (), s32[]{:S(2)}) async-start(), calls=%async_computation.1 | async-start | bytes 4718592 | tf_op jit(solution)/shard_map/reduce_scatter | solution.py:34
  12.2 63.1 %copy-start.1 = (f32[512,1,128]{2,1,0:T(1,128)S(1)}, f32[512,1,128]{2,1,0:T(1,128)}, u32[]{:S(2)}) copy-start(f32[512,1,128]{2,1,0:T(1,128)} %param.5) | copy-start | bytes 786436
  12.2 119.5 %all-reduce.2.cloned.1.call-start = ((), (), s32[]{:S(2)}) async-start(), calls=%async_computation.2 | async-start | bytes 131072 | tf_op jit(solution)/shard_map/psum | solution.py:48
  67.3 7.9 %collective-permute-start = (f32[512,128]{1,0:T(8,128)S(1)}, f32[512,128]{1,0:T(8,128)S(1)}, u32[]{:S(2)}, u32[]{:S(2)}) collective-permute-start(f32[512,128]{1,0:T(8,128)S(1)} %slice_select_fusion), channel_id=1, source_target_pairs={{0,1},{1,0},{2,3},{3,2},{4,5},{5,4},{6,7},{7,6},{8,9},{9,8},{10,11... | collective-permute-start | bytes 786440 | tf_op jit(solution)/shard_map/ppermute | solution.py:24
  131.7 4.5 %collective-permute-start.1 = (f32[128,128]{1,0:T(8,128)}, f32[128,128]{1,0:T(8,128)S(1)}, u32[]{:S(2)}, u32[]{:S(2)}) collective-permute-start(f32[128,128]{1,0:T(8,128)} %all-reduce.2.cloned.1.call-done), channel_id=1, source_target_pairs={{0,1},{1,0},{2,3},{3,2},{4,5},{5,4},{6,7},{7,6},{8,9},{9,8},{10,11... | collective-permute-start | bytes 196616 | tf_op jit(solution)/shard_map/ppermute | solution.py:24
Sparse Core Ops, SparseCore 0:
  12.4 53.8 reduce-scatter.1
  78.5 53.1 all-reduce.1
where the time goes:
time: 151 us
  waiting for transfers between devices  117 us (77%)
  between operations  14.9 us (10%)
  matrix products  9.86 us (7%)
  other arithmetic  4.35 us (3%)
  starting transfers between devices  3.11 us (2%)
  local copies, waits for them, and re-layouts  1.55 us (1%)
    reduce_scatter x1, waiting for transfers between devices, on_device(): lax.psum_scatter(lax.dot_general(features, own_part, contract, preferred_...  54 us
    psum x1, waiting for transfers between devices, on_device(): gram = lax.psum(gram, 'fsdp')  53.3 us
    ppermute x2, waiting for transfers between devices, swapped(): return lax.ppermute(block, axis, route)  9.37 us
    dot_general x1, matrix products, on_device(): lax.dot_general(features, own_part, contract, preferred_element_type=jnp....  3.45 us
    ppermute x2, starting transfers between devices, swapped(): return lax.ppermute(block, axis, route)  3.03 us
  transfers between devices with their start and end apart: 4, of which 4 were waited for; matrix products, arithmetic and copies ran while one was open for 0% of the time, Pallas kernels for 0%

commit v1 on v0

--- a/solution.py
+++ b/solution.py
@@ -45,7 +45,8 @@
     fresh = retain * moment + grads
     blend = grads + retain * fresh
     gram = lax.dot_general(blend, blend, contract, precision=precise)
-    gram = lax.psum(gram, "fsdp")
+    blocks = lax.all_gather(gram, "fsdp", axis=0, tiled=False)
+    gram = blocks.sum(axis=0)
     gram = gram + swapped(gram, "tp", 0)
     inverse = 1.0 / (jnp.sqrt(jnp.trace(gram)) + epsilon)
     state = blend * inverse

time: 151 us -> 106 us (0.70)
  waiting for transfers between devices: 117 us -> 63.3 us
  blocking collectives: 0 us -> 9.81 us
    psum x1 -> x0, waiting for transfers between devices: 53.3 us -> none  [on_device(): gram = lax.psum(gram, 'fsdp')]
    all_gather x0 -> x1, blocking collectives: none -> 9.81 us  [on_device(): blocks = lax.all_gather(gram, 'fsdp', axis=0, tiled=False)]
  transfers between devices with their start and end apart: 4 -> 3, of which waited for: 4 -> 3; matrix products, arithmetic and copies ran while one was open for 0% -> 0% of each run, Pallas kernels for 0% -> 0%
where the time goes in v1:
time: 106 us; the launch traced here: 105 us
  waiting for transfers between devices  63.3 us (60%)
  between operations  14.9 us (14%)
  blocking collectives  9.81 us (9%)
  matrix products  9.22 us (9%)
  other arithmetic  3.52 us (3%)
  starting transfers between devices  3.14 us (3%)
  local copies, waits for them, and re-layouts  1.55 us (1%)
    reduce_scatter x1, waiting for transfers between devices, on_device(): lax.psum_scatter(lax.dot_general(features, own_part, contract, preferred_...  54 us
    all_gather x1, blocking collectives, on_device(): blocks = lax.all_gather(gram, 'fsdp', axis=0, tiled=False)  9.81 us
    ppermute x2, waiting for transfers between devices, swapped(): return lax.ppermute(block, axis, route)  9.24 us
    dot_general x1, matrix products, on_device(): lax.dot_general(features, own_part, contract, preferred_element_type=jnp....  3.45 us
    ppermute x2, starting transfers between devices, swapped(): return lax.ppermute(block, axis, route)  3.1 us
    dot_general x5, matrix products, on_device(): state = jnp.dot(state, poly, precision=precise)  2.52 us
  transfers between devices with their start and end apart: 3, of which 3 were waited for; matrix products, arithmetic and copies ran while one was open for 0% of the time, Pallas kernels for 0%

profile of v1, /device:TPU:0, one launch (start us, length us, event | category | flops | bytes accessed | tf_op | source)
XLA Modules:
  0.0 105.5 jit_solution(10197081606354440241)
XLA Ops:
  7.2 0.0 reduce-scatter.2.cloned.1.call-start
  7.2 1.5 %copy-done = bf16[128,8192]{1,0:T(8,128)(2,1)S(1)} copy-done((bf16[128,8192]{1,0:T(8,128)(2,1)S(1)}, bf16[128,8192]{1,0:T(8,128)(2,1)}, u32[]{:S(2)}) %copy-start) | copy-done | bytes 2097176
  8.8 3.4 %fusion.14 = f32[8192,128]{1,0:T(8,128)} fusion(bf16[128,8192]{1,0:T(8,128)(2,1)S(1)} %copy-done, bf16[128,1,128]{2,0,1:T(8,128)(2,1)} %param.4), kind=kOutput, calls=%fused_computation.29 | convolution fusion | flops 268435456 | bytes 6324224 | tf_op jit(solution)/shard_map/dot_general | solution.py:35
  12.2 0.0 reduce-scatter.2.cloned.1.call-update
  12.2 54.0 %reduce-scatter.2.cloned.1.call-done = f32[1024,128]{1,0:T(8,128)} async-done(((f32[8192,128]{1,0:T(8,128)}), f32[1024,128]{1,0:T(8,128)}) %reduce-scatter.2.cloned.1.call-update) | async-done | bytes 524304 | tf_op jit(solution)/shard_map/reduce_scatter | solution.py:34
  66.3 1.1 %slice_select_fusion = f32[512,128]{1,0:T(8,128)S(1)} fusion(f32[1024,128]{1,0:T(8,128)} %reduce-scatter.2.cloned.1.call-done, pred[]{:T(512)S(6)} %eq.21), kind=kLoop, calls=%fused_computation.15 | loop fusion | flops 65536 | bytes 786433 | tf_op jit(solution)/shard_map/jit(_where)/select_n | solution.py:42
  67.3 1.5 %collective-permute-start = (f32[512,128]{1,0:T(8,128)S(1)}, f32[512,128]{1,0:T(8,128)S(1)}, u32[]{:S(2)}, u32[]{:S(2)}) collective-permute-start(f32[512,128]{1,0:T(8,128)S(1)} %slice_select_fusion), channel_id=1, source_target_pairs={{0,1},{1,0},{2,3},{3,2},{4,5},{5,4},{6,7},{7,6},{8,9},{9,8},{10,11... | collective-permute-start | bytes 786440 | tf_op jit(solution)/shard_map/ppermute | solution.py:24
  68.9 6.4 %collective-permute-done = f32[512,128]{1,0:T(8,128)S(1)} collective-permute-done((f32[512,128]{1,0:T(8,128)S(1)}, f32[512,128]{1,0:T(8,128)S(1)}, u32[]{:S(2)}, u32[]{:S(2)}) %collective-permute-start) | collective-permute-done | bytes 262176 | tf_op jit(solution)/shard_map/ppermute | solution.py:24
  75.3 1.8 %bitcast_add_fusion = (f32[512,128]{1,0:T(8,128)}, f32[512,128]{1,0:T(8,128)S(1)}) fusion(f32[512,1,128]{2,0,1:T(8,128)S(1)} %bitcast.52, f32[512,128]{1,0:T(8,128)S(1)} %collective-permute-done, f32[1024,128]{1,0:T(8,128)} %reduce-scatter.2.cloned.1.call-done, pred[]{:T(512)S(6)} %eq.21), kind=kLoop, calls=%fused_computation.10 | loop fusion | flops 262144 | bytes 1572865 | tf_op jit(solution)/shard_map/add | solution.py:45
  77.1 0.6 fusion.7
  77.7 9.8 %all-gather = f32[1024,128]{1,0:T(8,128)S(1)} all-gather(f32[128,128]{1,0:T(8,128)S(1)} %fusion.7), channel_id=2, replica_groups=mesh['fsdp'=8,'tp'=4] {'fsdp'}, dimensions={0}, use_global_device_ids=true | all-gather | bytes 589824 | tf_op jit(solution)/shard_map/all_gather | solution.py:48
  87.5 1.6 %collective-permute-start.1 = (f32[128,128]{1,0:T(8,128)S(1)}, f32[128,128]{1,0:T(8,128)S(1)}, u32[]{:S(2)}, u32[]{:S(2)}) collective-permute-start(f32[128,128]{1,0:T(8,128)S(1)} %reduce_sum.19), channel_id=1, source_target_pairs={{0,1},{1,0},{2,3},{3,2},{4,5},{5,4},{6,7},{7,6},{8,9},{9,8},{10,11... | collective-permute-start | bytes 196616 | tf_op jit(solution)/shard_map/ppermute | solution.py:24
  89.1 2.9 %collective-permute-done.1 = f32[128,128]{1,0:T(8,128)S(1)} collective-permute-done((f32[128,128]{1,0:T(8,128)S(1)}, f32[128,128]{1,0:T(8,128)S(1)}, u32[]{:S(2)}, u32[]{:S(2)}) %collective-permute-start.1) | collective-permute-done | bytes 65568 | tf_op jit(solution)/shard_map/ppermute | solution.py:24
  92.0 0.6 select_reduce_fusion
  93.3 0.2 fusion.8
  93.5 0.4 fusion.4
  93.9 0.2 fusion.9
  94.1 0.2 fusion.20
  94.3 0.2 fusion.3
  94.5 0.2 fusion.22
  94.7 0.4 fusion.21
  95.1 0.2 fusion.23
  95.3 0.2 fusion.2
  95.5 0.2 fusion.25
  95.7 0.4 fusion.24
  96.1 0.2 fusion.26
  96.3 0.2 fusion.1
  96.5 0.2 fusion.28
  96.7 0.4 fusion.27
  97.1 0.2 fusion.29
  97.3 0.2 fusion
  97.5 1.1 %convolution_multiply_fusion = f32[512,128]{1,0:T(8,128)} fusion(f32[512,128]{1,0:T(8,128)S(1)} %fusion.27, f32[128,128]{1,0:T(8,128)S(1)} %fusion), kind=kOutput, calls=%fused_computation | convolution fusion | flops 100728832 | bytes 589824 | tf_op jit(solution)/shard_map/dot_general | solution.py:58
  (4 shorter events, 0.0 us)
Async XLA Ops:
  7.2 1.6 %copy-start = (bf16[128,8192]{1,0:T(8,128)(2,1)S(1)}, bf16[128,8192]{1,0:T(8,128)(2,1)}, u32[]{:S(2)}) copy-start(bf16[128,8192]{1,0:T(8,128)(2,1)} %param.3) | copy-start | bytes 6291460
  7.2 59.1 %reduce-scatter.2.cloned.1.call-start = ((), (), s32[]{:S(2)}) async-start(), calls=%async_computation.1 | async-start | bytes 4718592 | tf_op jit(solution)/shard_map/reduce_scatter | solution.py:34
  12.2 63.1 %copy-start.1 = (f32[512,1,128]{2,1,0:T(1,128)S(1)}, f32[512,1,128]{2,1,0:T(1,128)}, u32[]{:S(2)}) copy-start(f32[512,1,128]{2,1,0:T(1,128)} %param.5) | copy-start | bytes 786436
  67.3 7.9 %collective-permute-start = (f32[512,128]{1,0:T(8,128)S(1)}, f32[512,128]{1,0:T(8,128)S(1)}, u32[]{:S(2)}, u32[]{:S(2)}) collective-permute-start(f32[512,128]{1,0:T(8,128)S(1)} %slice_select_fusion), channel_id=1, source_target_pairs={{0,1},{1,0},{2,3},{3,2},{4,5},{5,4},{6,7},{7,6},{8,9},{9,8},{10,11... | collective-permute-start | bytes 786440 | tf_op jit(solution)/shard_map/ppermute | solution.py:24
  87.5 4.4 %collective-permute-start.1 = (f32[128,128]{1,0:T(8,128)S(1)}, f32[128,128]{1,0:T(8,128)S(1)}, u32[]{:S(2)}, u32[]{:S(2)}) collective-permute-start(f32[128,128]{1,0:T(8,128)S(1)} %reduce_sum.19), channel_id=1, source_target_pairs={{0,1},{1,0},{2,3},{3,2},{4,5},{5,4},{6,7},{7,6},{8,9},{9,8},{10,11... | collective-permute-start | bytes 196616 | tf_op jit(solution)/shard_map/ppermute | solution.py:24
Sparse Core Ops, SparseCore 0:
  12.4 53.8 reduce-scatter.1
